TPU v7x, 32 devices: a whole 2x2x4 slice. The times are simulated.
32 devices in a mesh: rep: 8 (over z, y), grp: 4 (over x, core).
Axes of the slice: x: 2, y: 2, z: 4, core: 2. Of those that a mesh axis runs over, the one named last changes fastest.
Arguments:
- tokens: bfloat16 [3648, 1152], P(('rep', 'grp')), may hold values from -6 to 6
- cotangent: bfloat16 [3648, 1152], P(('rep', 'grp')), may hold values from -6 to 6
- slice_sizes: int32 [32], replicated, may hold values from 113 to 114, as said below
- gain_one: float32 [1152], replicated, may hold values from 0.1 to 1.9
- shift_one: float32 [1152], replicated, may hold values from -3 to 3
- attn_in: bfloat16 [3456, 1152], P('grp')
- attn_bias: float32 [2, 1152], replicated, may hold values from -3 to 3
- attn_out: bfloat16 [1152, 1152], P('grp'), may hold values from -1 to 1
- out_bias: float32 [1152], replicated, may hold values from -3 to 3
- gain_two: float32 [1152], replicated, may hold values from 0.1 to 1.9
- shift_two: float32 [1152], replicated, may hold values from -3 to 3
- mlp_up: bfloat16 [4304, 1152], P('grp'), may hold values from -0.1875 to 0.1875
- up_bias: float32 [4304], replicated, may hold values from -3 to 3
- mlp_down: bfloat16 [4304, 1152], P('grp'), may hold values from -0.09375 to 0.09375
- down_bias: float32 [1152], replicated, may hold values from -3 to 3
Outputs:
- block_output: bfloat16 [3648, 1152], P(('rep', 'grp'))
- input_grad: float32 [3648, 1152], P(('rep', 'grp'))
- dgain_one: float32 [1152], replicated
- dshift_one: float32 [1152], replicated
- dattn_in: float32 [3456, 1152], P('grp', 'rep')
- dattn_bias: float32 [2, 1152], replicated
- dattn_out: float32 [1152, 1152], P('grp', 'rep')
- dout_bias: float32 [1152], replicated
- dgain_two: float32 [1152], replicated
- dshift_two: float32 [1152], replicated
- dmlp_up: float32 [4304, 1152], P('grp', 'rep')
- dup_bias: float32 [4304], replicated
- dmlp_down: float32 [4304, 1152], P('grp', 'rep')
- ddown_bias: float32 [1152], replicated
Inputs may be any that keep to these rules, and one draw needn't show every extreme that they name: slice_sizes sums to 3645; every entry is 113 or one more.
All inputs are finite; a program needn't handle non-finite values.
Results may differ from a plain program's by a relative error of at most 0.012.
Values may be sent and summed in bfloat16 or wider, within the bound.
A program may use at most 192 MiB of HBM per device.

v0:
```python
import jax
import jax.numpy as jnp
from jax import lax
from jax.sharding import PartitionSpec as P

H = 16
HD = 72
IMG = 729
EPSILON = 1e-06
SQRT_TWO_PI = 0.7978845608028654
CUBIC = 0.044715
NEGATIVE = -1e30


def passed_along(block, axis, distance):
    devices = range(lax.axis_size(axis))
    route = [(i - distance, i) for i in devices if i - distance in devices]
    return lax.ppermute(block, axis, route)


def norm_forward(rows, gain_row, shift_row):
    centered = rows - jnp.mean(rows, axis=-1, keepdims=True)
    inverse = lax.rsqrt(jnp.mean(centered * centered, axis=-1, keepdims=True) + EPSILON)
    normed = centered * inverse
    return (normed, inverse, normed * gain_row + shift_row)


def norm_backward(dscaled, normed, inverse, gain_row):
    dnormed = dscaled * gain_row
    return inverse * (
        dnormed
        - jnp.mean(dnormed, axis=-1, keepdims=True)
        - normed * jnp.mean(dnormed * normed, axis=-1, keepdims=True)
    )


def gelu_parts(before):
    inside = SQRT_TWO_PI * (before + CUBIC * before * before * before)
    tangent = jnp.tanh(inside)
    activated = 0.5 * before * (1.0 + tangent)
    derivative = 0.5 * (1.0 + tangent) + 0.5 * before * (1.0 - tangent * tangent) * SQRT_TWO_PI * (
        1.0 + 3.0 * CUBIC * before * before
    )
    return (activated, derivative)


def owned_grads(left_one, right_one, left_two, right_two):
    all_left_one, all_right_one, all_left_two, all_right_two = (
        lax.all_gather(left_one, "grp", axis=0, tiled=True),
        lax.all_gather(right_one, "grp", axis=0, tiled=True),
        lax.all_gather(left_two, "grp", axis=0, tiled=True),
        lax.all_gather(right_two, "grp", axis=0, tiled=True),
    )
    member = lax.axis_index("grp")
    groups = lax.axis_size("grp")
    rows_one = left_one.shape[1] // groups
    rows_two = left_two.shape[1] // groups
    picked_one = lax.dynamic_slice_in_dim(all_left_one, member * rows_one, rows_one, 1)
    picked_two = lax.dynamic_slice_in_dim(all_left_two, member * rows_two, rows_two, 1)
    grad_one = jnp.dot(picked_one.T, all_right_one, preferred_element_type=jnp.float32)
    grad_two = jnp.dot(picked_two.T, all_right_two, preferred_element_type=jnp.float32)
    return (grad_one, grad_two)


def replica_sums(first_rows, second_rows):
    return (
        lax.psum_scatter(first_rows, "rep", scatter_dimension=1, tiled=True),
        lax.psum_scatter(second_rows, "rep", scatter_dimension=1, tiled=True),
    )


def per_device(
    tokens,
    cotangent,
    slice_sizes,
    gain_one,
    shift_one,
    attn_in,
    attn_bias,
    attn_out,
    out_bias,
    gain_two,
    shift_two,
    mlp_up,
    up_bias,
    mlp_down,
    down_bias,
):
    capacity, width = tokens.shape
    base_rows = capacity - 1
    reach = (IMG - 2 + base_rows) // base_rows
    windows = (capacity + IMG - 2) // IMG + 1
    window_keys = windows * IMG
    score_scale = HD ** (-0.5)
    device = lax.axis_index(("rep", "grp"))
    starts = jnp.cumsum(slice_sizes) - slice_sizes
    own_start = starts[device]
    own_count = slice_sizes[device]
    row_index = jnp.arange(capacity, dtype=jnp.int32)
    is_live = row_index < own_count
    live_col = is_live[:, None]
    query_image = (own_start + row_index) // IMG
    first_image = own_start // IMG
    last_image = (own_start + own_count - 1) // IMG
    window_image = first_image + jnp.arange(windows, dtype=jnp.int32)
    key_image = jnp.repeat(jnp.minimum(window_image, last_image), IMG)
    key_live = jnp.repeat(window_image <= last_image, IMG)
    key_place = key_image * IMG + jnp.tile(jnp.arange(IMG, dtype=jnp.int32), windows)
    earlier = starts[None, :] <= key_place[:, None]
    owner = jnp.sum(earlier.astype(jnp.int32), axis=1) - 1
    owner_start = jnp.max(jnp.where(earlier, starts[None, :], 0), axis=1)
    buffer_row = (owner - device + reach) * capacity + key_place - owner_start
    allowed = (query_image[:, None] == key_image[None, :]) & key_live[None, :] & live_col
    full_in, full_out, full_up, full_down = (
        lax.all_gather(attn_in, "grp", axis=0, tiled=True),
        lax.all_gather(attn_out, "grp", axis=0, tiled=True),
        lax.all_gather(mlp_up, "grp", axis=0, tiled=True),
        lax.all_gather(mlp_down, "grp", axis=0, tiled=True),
    )
    tokens_f = tokens.astype(jnp.float32)
    normed_one, inverse_one, scaled_one = norm_forward(tokens_f, gain_one, shift_one)
    first = scaled_one.astype(jnp.bfloat16)
    bias_full = jnp.concatenate([attn_bias[0], jnp.zeros((width,), jnp.float32), attn_bias[1]])
    projected = jnp.dot(first, full_in.T, preferred_element_type=jnp.float32) + bias_full
    queries = projected[:, :width].astype(jnp.bfloat16)
    keyvalue = projected[:, width:].astype(jnp.bfloat16)
    pieces = []
    for offset in range(-reach, reach + 1):
        if offset == 0:
            pieces.append(keyvalue)
        else:
            pieces.append(passed_along(keyvalue, ("rep", "grp"), -offset))
    neighbours = jnp.concatenate(pieces, axis=0)
    window = neighbours[buffer_row]
    keys3 = window[:, :width].reshape(window_keys, H, HD)
    values3 = window[:, width:].reshape(window_keys, H, HD)
    queries3 = queries.reshape(capacity, H, HD)

    def masked_scores():
        raw = (
            jnp.einsum("qhd,khd->hqk", queries3, keys3, preferred_element_type=jnp.float32)
            * score_scale
        )
        return jnp.where(allowed[None], raw, NEGATIVE)

    scores = masked_scores()
    highest = jnp.max(scores, axis=-1, keepdims=True)
    logsum = highest + jnp.log(jnp.sum(jnp.exp(scores - highest), axis=-1, keepdims=True))
    weights = jnp.where(allowed[None], jnp.exp(scores - logsum), 0.0).astype(jnp.bfloat16)
    mixed = (
        jnp.einsum("hqk,khd->qhd", weights, values3, preferred_element_type=jnp.float32)
        .astype(jnp.bfloat16)
        .reshape(capacity, width)
    )
    resid = tokens_f + jnp.dot(mixed, full_out, preferred_element_type=jnp.float32) + out_bias
    normed_two, inverse_two, scaled_two = norm_forward(resid, gain_two, shift_two)
    second = scaled_two.astype(jnp.bfloat16)
    before = jnp.dot(second, full_up.T, preferred_element_type=jnp.float32) + up_bias
    activated, derivative = gelu_parts(before)
    hidden = activated.astype(jnp.bfloat16)
    final = resid + jnp.dot(hidden, full_down, preferred_element_type=jnp.float32) + down_bias
    block_output = jnp.where(live_col, final, 0.0).astype(jnp.bfloat16)
    dfinal_b = jnp.where(live_col, cotangent, jnp.zeros_like(cotangent))
    dfinal = dfinal_b.astype(jnp.float32)
    dbefore = jnp.dot(dfinal_b, full_down.T, preferred_element_type=jnp.float32) * derivative
    dbefore_b = dbefore.astype(jnp.bfloat16)
    dsecond = jnp.dot(dbefore_b, full_up, preferred_element_type=jnp.float32)
    dresid = dfinal + norm_backward(dsecond, normed_two, inverse_two, gain_two)
    mlp_up_rows, mlp_down_rows = owned_grads(dbefore_b, second, hidden, dfinal_b)
    dmlp_up, dmlp_down = replica_sums(mlp_up_rows, mlp_down_rows)
    dresid_b = dresid.astype(jnp.bfloat16)
    dmixed = jnp.dot(dresid_b, full_out.T, preferred_element_type=jnp.float32).astype(jnp.bfloat16)
    dmixed3 = dmixed.reshape(capacity, H, HD)
    delta = jnp.sum(
        dmixed3.astype(jnp.float32) * mixed.reshape(capacity, H, HD).astype(jnp.float32), axis=-1
    ).T
    scores = masked_scores()
    probs = jnp.where(allowed[None], jnp.exp(scores - logsum), 0.0)
    dprob = jnp.einsum("qhd,khd->hqk", dmixed3, values3, preferred_element_type=jnp.float32)
    dscore = (probs * (dprob - delta[:, :, None]) * score_scale).astype(jnp.bfloat16)
    dquery = jnp.einsum("hqk,khd->qhd", dscore, keys3, preferred_element_type=jnp.float32).reshape(
        capacity, width
    )
    dkey = jnp.einsum("hqk,qhd->khd", dscore, queries3, preferred_element_type=jnp.float32).reshape(
        window_keys, width
    )
    dvalue = jnp.einsum(
        "hqk,qhd->khd", weights, dmixed3, preferred_element_type=jnp.float32
    ).reshape(window_keys, width)
    dwindow = jnp.concatenate([dkey, dvalue], axis=1)
    dneighbours = (
        jnp.zeros((neighbours.shape[0], 2 * width), jnp.float32).at[buffer_row].add(dwindow)
    )
    dkeyvalue = dneighbours[reach * capacity : (reach + 1) * capacity]
    for offset in range(-reach, reach + 1):
        if offset != 0:
            segment = dneighbours[(offset + reach) * capacity : (offset + reach + 1) * capacity]
            dkeyvalue = dkeyvalue + passed_along(segment, ("rep", "grp"), offset)
    dprojected = jnp.concatenate([dquery, dkeyvalue], axis=1).astype(jnp.bfloat16)
    attn_in_rows, attn_out_rows = owned_grads(dprojected, first, mixed, dresid_b)
    dattn_in, dattn_out = replica_sums(attn_in_rows, attn_out_rows)
    dfirst = jnp.dot(dprojected, full_in, preferred_element_type=jnp.float32)
    input_grad = jnp.where(
        live_col, dresid + norm_backward(dfirst, normed_one, inverse_one, gain_one), 0.0
    )
    dgain_one, dshift_one, dattn_bias, dout_bias, dgain_two, dshift_two, dup_bias, ddown_bias = (
        lax.psum(
            (
                jnp.sum(dfirst * normed_one, axis=0),
                jnp.sum(dfirst, axis=0),
                jnp.stack([jnp.sum(dquery, axis=0), jnp.sum(dkeyvalue[:, width:], axis=0)]),
                jnp.sum(dresid, axis=0),
                jnp.sum(dsecond * normed_two, axis=0),
                jnp.sum(dsecond, axis=0),
                jnp.sum(dbefore, axis=0),
                jnp.sum(dfinal, axis=0),
            ),
            ("rep", "grp"),
        )
    )
    return (
        block_output,
        input_grad,
        dgain_one,
        dshift_one,
        dattn_in,
        dattn_bias,
        dattn_out,
        dout_bias,
        dgain_two,
        dshift_two,
        dmlp_up,
        dup_bias,
        dmlp_down,
        ddown_bias,
    )


def solution(mesh):
    in_specs = (
        P(("rep", "grp"), None),
        P(("rep", "grp"), None),
        P(),
        P(),
        P(),
        P("grp", None),
        P(),
        P("grp", None),
        P(),
        P(),
        P(),
        P("grp", None),
        P(),
        P("grp", None),
        P(),
    )
    out_specs = (
        P(("rep", "grp"), None),
        P(("rep", "grp"), None),
        P(),
        P(),
        P("grp", "rep"),
        P(),
        P("grp", "rep"),
        P(),
        P(),
        P(),
        P("grp", "rep"),
        P(),
        P("grp", "rep"),
        P(),
    )
    return jax.shard_map(
        per_device, mesh=mesh, in_specs=in_specs, out_specs=out_specs, check_vma=False
    )
```

profile of v0, /device:TPU:0, one launch (start us, length us, event | category | flops | bytes accessed | tf_op | source)
XLA Modules:
  0.0 1322.7 jit_solution(18031253088932466341)
XLA Ops:
  15.5 52.6 %all-gather.23.cloned.1.call-done = bf16[3456,1152]{1,0:T(8,128)(2,1)} async-done(((bf16[864,1152]{1,0:T(8,128)(2,1)}), bf16[3456,1152]{1,0:T(8,128)(2,1)}) %all-gather.23.cloned.1.call-update) | async-done | bytes 7962640 | tf_op jit(solution)/shard_map/all_gather | solution.py:115
  81.3 20.4 %collective-permute-done.13 = bf16[114,2304]{1,0:T(8,128)(2,1)S(1)} collective-permute-done((bf16[114,2304]{1,0:T(8,128)(2,1)S(1)}, bf16[114,2304]{1,0:T(8,128)(2,1)S(1)}, u32[]{:S(2)}, u32[]{:S(2)}) %collective-permute-start.13) | collective-permute-done | bytes 525344 | tf_op jit(solution)/shard_map/ppermute | solution.py:18
  106.9 13.9 %collective-permute-start.6 = (bf16[114,2304]{1,0:T(8,128)(2,1)S(1)}, bf16[114,2304]{1,0:T(8,128)(2,1)S(1)}, u32[]{:S(2)}, u32[]{:S(2)}) collective-permute-start(bf16[114,2304]{1,0:T(8,128)(2,1)S(1)} %slice.92), channel_id=1, source_target_pairs={{0,1},{1,2},{2,3},{3,4},{4,5},{5,6},{6,7},{7,8},{8,9},{9,10},{10,1... | collective-permute-start | bytes 1575944 | tf_op jit(solution)/shard_map/ppermute | solution.py:18
  134.1 17.2 %collective-permute-start.3 = (bf16[114,2304]{1,0:T(8,128)(2,1)S(1)}, bf16[114,2304]{1,0:T(8,128)(2,1)}, u32[]{:S(2)}, u32[]{:S(2)}) collective-permute-start(bf16[114,2304]{1,0:T(8,128)(2,1)S(1)} %slice.92), channel_id=1, source_target_pairs={{0,4},{1,5},{2,6},{3,7},{4,8},{5,9},{6,10},{7,11},{8,12},{9,13},{1... | collective-permute-start | bytes 1575944 | tf_op jit(solution)/shard_map/ppermute | solution.py:18
  155.1 28.5 %collective-permute-start.1 = (bf16[114,2304]{1,0:T(8,128)(2,1)S(1)}, bf16[114,2304]{1,0:T(8,128)(2,1)}, u32[]{:S(2)}, u32[]{:S(2)}) collective-permute-start(bf16[114,2304]{1,0:T(8,128)(2,1)S(1)} %slice.92), channel_id=1, source_target_pairs={{0,6},{1,7},{2,8},{3,9},{4,10},{5,11},{6,12},{7,13},{8,14},{9,15},... | collective-permute-start | bytes 1575944 | tf_op jit(solution)/shard_map/ppermute | solution.py:18
  194.2 19.5 %collective-permute-done.1 = bf16[114,2304]{1,0:T(8,128)(2,1)} collective-permute-done((bf16[114,2304]{1,0:T(8,128)(2,1)S(1)}, bf16[114,2304]{1,0:T(8,128)(2,1)}, u32[]{:S(2)}, u32[]{:S(2)}) %collective-permute-start.1) | collective-permute-done | bytes 525344 | tf_op jit(solution)/shard_map/ppermute | solution.py:18
  213.7 21.3 %collective-permute-done = bf16[114,2304]{1,0:T(8,128)(2,1)} collective-permute-done((bf16[114,2304]{1,0:T(8,128)(2,1)S(1)}, bf16[114,2304]{1,0:T(8,128)(2,1)}, u32[]{:S(2)}, u32[]{:S(2)}) %collective-permute-start) | collective-permute-done | bytes 525344 | tf_op jit(solution)/shard_map/ppermute | solution.py:18
  235.0 57.9 %concatenate.14 = bf16[1710,2304]{1,0:T(8,128)(2,1)} concatenate(bf16[114,2304]{1,0:T(8,128)(2,1)} %collective-permute-done, bf16[114,2304]{1,0:T(8,128)(2,1)} %collective-permute-done.1, bf16[114,2304]{1,0:T(8,128)(2,1)} %collective-permute-done.2, bf16[114,2304]{1,0:T(8,128)(2,1)} %collective-permute-done.3, bf16[114,2304]{1,0:T(8,128)(2,1)} %collective-permute-done.4, ...), dimensions={0} | concatenate | bytes 15759360 | tf_op jit(solution)/shard_map/concatenate | solution.py:133
  292.9 18.3 %gather_fusion = bf16[1458,2304]{1,0:T(8,128)(2,1)} fusion(bf16[1710,2304]{1,0:T(8,128)(2,1)} %concatenate.14, s32[2048]{0:T(1024)S(1)} %pad_clamp_fusion), kind=kCustom, calls=%fused_computation | custom fusion | bytes 13442760 | tf_op jit(solution)/shard_map/gather | solution.py:134
  438.1 29.8 %scatter_custom_fusion = f32[1710,2304]{1,0:T(8,128)} fusion(s32[1458]{0:T(1024)} %copy-done.35, f32[1458,1152]{1,0:T(8,128)} %copy.60, f32[]{:T(128)} %constant.83.clone.1, f32[1458,1152]{1,0:T(8,128)} %copy.59, f32[]{:T(128)} %constant.37.clone.1), kind=kCustom, calls=%fused_computation.2 | custom fusion | flops 6718464 | bytes 29252608 | tf_op jit(solution)/shard_map/scatter-add | solution.py:192
  498.5 13.1 collective-permute-done.27
  513.8 21.4 %collective-permute-done.26 = f32[114,2304]{1,0:T(8,128)S(1)} collective-permute-done((f32[114,2304]{1,0:T(8,128)S(1)}, f32[114,2304]{1,0:T(8,128)S(1)}, u32[]{:S(2)}, u32[]{:S(2)}) %collective-permute-start.26) | collective-permute-done | bytes 1050656 | tf_op jit(solution)/shard_map/ppermute | solution.py:18
  537.6 15.8 %collective-permute-done.25 = f32[114,2304]{1,0:T(8,128)S(1)} collective-permute-done((f32[114,2304]{1,0:T(8,128)S(1)}, f32[114,2304]{1,0:T(8,128)S(1)}, u32[]{:S(2)}, u32[]{:S(2)}) %collective-permute-start.25) | collective-permute-done | bytes 1050656 | tf_op jit(solution)/shard_map/ppermute | solution.py:18
  556.7 20.5 %collective-permute-done.24 = f32[114,2304]{1,0:T(8,128)} collective-permute-done((f32[114,2304]{1,0:T(8,128)}, f32[114,2304]{1,0:T(8,128)}, u32[]{:S(2)}, u32[]{:S(2)}) %collective-permute-start.24) | collective-permute-done | bytes 1050656 | tf_op jit(solution)/shard_map/ppermute | solution.py:18
  579.8 32.6 %collective-permute-done.22 = f32[114,2304]{1,0:T(8,128)} collective-permute-done((f32[114,2304]{1,0:T(8,128)}, f32[114,2304]{1,0:T(8,128)}, u32[]{:S(2)}, u32[]{:S(2)}) %collective-permute-start.22) | collective-permute-done | bytes 1050656 | tf_op jit(solution)/shard_map/ppermute | solution.py:18
  635.0 61.3 %collective-permute-done.17 = f32[114,2304]{1,0:T(8,128)} collective-permute-done((f32[114,2304]{1,0:T(8,128)}, f32[114,2304]{1,0:T(8,128)}, u32[]{:S(2)}, u32[]{:S(2)}) %collective-permute-start.17) | collective-permute-done | bytes 1050656 | tf_op jit(solution)/shard_map/ppermute | solution.py:18
  724.3 72.8 %all-gather.33.cloned.1.call-done = bf16[4,114,1152]{2,1,0:T(8,128)(2,1)} async-done(((bf16[1,114,1152]{2,1,0:T(8,128)(2,1)}), bf16[4,114,1152]{2,1,0:T(8,128)(2,1)}) %all-gather.33.cloned.1.call-update) | async-done | bytes 1050640 | tf_op jit(solution)/shard_map/all_gather | solution.py:50
  799.7 28.5 %all-gather.31.cloned.1.call-done = bf16[4,114,3456]{2,1,0:T(8,128)(2,1)} async-done(((bf16[1,114,3456]{2,1,0:T(8,128)(2,1)}), bf16[4,114,3456]{2,1,0:T(8,128)(2,1)}) %all-gather.31.cloned.1.call-update) | async-done | bytes 3151888 | tf_op jit(solution)/shard_map/all_gather | solution.py:49
  848.9 34.3 %all-gather.43.cloned.1.call-done = bf16[4,114,4304]{2,1,0:T(8,128)(2,1)} async-done(((bf16[1,114,4304]{2,1,0:T(8,128)(2,1)}), bf16[4,114,4304]{2,1,0:T(8,128)(2,1)}) %all-gather.43.cloned.1.call-update) | async-done | bytes 3925264 | tf_op jit(solution)/shard_map/all_gather | solution.py:51
  903.9 34.3 %all-gather.39.cloned.1.call-done = bf16[4,114,4304]{2,1,0:T(8,128)(2,1)} async-done(((bf16[1,114,4304]{2,1,0:T(8,128)(2,1)}), bf16[4,114,4304]{2,1,0:T(8,128)(2,1)}) %all-gather.39.cloned.1.call-update) | async-done | bytes 3925264 | tf_op jit(solution)/shard_map/all_gather | solution.py:49
  958.0 42.1 %all-reduce = (f32[1152]{0:T(1024)}, f32[1152]{0:T(1024)}, f32[2,1152]{1,0:T(2,128)}, f32[1152]{0:T(1024)}, f32[1152]{0:T(1024)}, /*index=5*/f32[1152]{0:T(1024)}, f32[4304]{0:T(1024)}, f32[1152]{0:T(1024)}) all-reduce(f32[1152]{0:T(1024)S(1)} %get-tuple-element.16, ...), channel_id=1, replica_groups=mesh['rep'=8,'grp'=4] {'rep','grp'}, use_global_device_ids=true, to_apply=%region_16.17 | all-reduce | flops 13520 | bytes 108160 | tf_op jit(solution)/shard_map/psum | solution.py:207
  1009.0 90.7 %reduce-scatter.5.cloned.1.call-done = f32[864,144]{0,1:T(8,128)} async-done(((f32[864,1152]{0,1:T(8,128)}), f32[864,144]{0,1:T(8,128)}) %reduce-scatter.5.cloned.1.call-update) | async-done | bytes 497680 | tf_op jit(solution)/shard_map/reduce_scatter | solution.py:67
  1099.7 108.1 %reduce-scatter.11.cloned.1.call-done = f32[1076,144]{0,1:T(8,128)} async-done(((f32[1076,1152]{0,1:T(8,128)}), f32[1076,144]{0,1:T(8,128)}) %reduce-scatter.11.cloned.1.call-update) | async-done | bytes 619792 | tf_op jit(solution)/shard_map/reduce_scatter | solution.py:68
  1207.8 108.2 %reduce-scatter.9.cloned.1.call-done = f32[1076,144]{0,1:T(8,128)} async-done(((f32[1076,1152]{0,1:T(8,128)}), f32[1076,144]{0,1:T(8,128)}) %reduce-scatter.9.cloned.1.call-update) | async-done | bytes 619792 | tf_op jit(solution)/shard_map/reduce_scatter | solution.py:67
  (291 shorter events, 341.1 us)
Async XLA Ops:
  7.9 333.9 %all-gather.25.cloned.1.call-start = ((), (), s32[]{:S(2)}) async-start(), calls=%async_computation.5 | async-start | bytes 3317760 | tf_op jit(solution)/shard_map/all_gather | solution.py:116
  8.7 336.1 %all-gather.27.cloned.1.call-start = ((), (), s32[]{:S(2)}) async-start(), calls=%async_computation.10 | async-start | bytes 12441600 | tf_op jit(solution)/shard_map/all_gather | solution.py:117
  9.4 354.1 %all-gather.29.cloned.1.call-start = ((), (), s32[]{:S(2)}) async-start(), calls=%async_computation.11 | async-start | bytes 12441600 | tf_op jit(solution)/shard_map/all_gather | solution.py:118
  10.0 708.9 %all-gather.35.cloned.1.call-start = ((), (), s32[]{:S(2)}) async-start(), calls=%async_computation.14 | async-start | bytes 1382400 | tf_op jit(solution)/shard_map/all_gather | solution.py:51
  128.2 66.0 %collective-permute-start.4 = (bf16[114,2304]{1,0:T(8,128)(2,1)S(1)}, bf16[114,2304]{1,0:T(8,128)(2,1)}, u32[]{:S(2)}, u32[]{:S(2)}) collective-permute-start(bf16[114,2304]{1,0:T(8,128)(2,1)S(1)} %slice.92), channel_id=1, source_target_pairs={{0,3},{1,4},{2,5},{3,6},{4,7},{5,8},{6,9},{7,10},{8,11},{9,12},{10... | collective-permute-start | bytes 1575944 | tf_op jit(solution)/shard_map/ppermute | solution.py:18
  486.5 66.9 %collective-permute-start.25 = (f32[114,2304]{1,0:T(8,128)S(1)}, f32[114,2304]{1,0:T(8,128)S(1)}, u32[]{:S(2)}, u32[]{:S(2)}) collective-permute-start(f32[114,2304]{1,0:T(8,128)S(1)} %get-tuple-element.43), channel_id=1, source_target_pairs={{0,5},{1,6},{2,7},{3,8},{4,9},{5,10},{6,11},{7,12},{8,13},{9,14},{... | collective-permute-start | bytes 3151880 | tf_op jit(solution)/shard_map/ppermute | solution.py:18
  487.9 89.3 %collective-permute-start.24 = (f32[114,2304]{1,0:T(8,128)}, f32[114,2304]{1,0:T(8,128)}, u32[]{:S(2)}, u32[]{:S(2)}) collective-permute-start(f32[114,2304]{1,0:T(8,128)} %get-tuple-element.44), channel_id=1, source_target_pairs={{0,4},{1,5},{2,6},{3,7},{4,8},{5,9},{6,10},{7,11},{8,12},{9,13},{1... | collective-permute-start | bytes 3151880 | tf_op jit(solution)/shard_map/ppermute | solution.py:18
  496.2 82.3 %collective-permute-start.23 = (f32[114,2304]{1,0:T(8,128)}, f32[114,2304]{1,0:T(8,128)}, u32[]{:S(2)}, u32[]{:S(2)}) collective-permute-start(f32[114,2304]{1,0:T(8,128)} %get-tuple-element.45), channel_id=1, source_target_pairs={{0,3},{1,4},{2,5},{3,6},{4,7},{5,8},{6,9},{7,10},{8,11},{9,12},{10... | collective-permute-start | bytes 3151880 | tf_op jit(solution)/shard_map/ppermute | solution.py:18
  511.6 100.8 %collective-permute-start.22 = (f32[114,2304]{1,0:T(8,128)}, f32[114,2304]{1,0:T(8,128)}, u32[]{:S(2)}, u32[]{:S(2)}) collective-permute-start(f32[114,2304]{1,0:T(8,128)} %get-tuple-element.46), channel_id=1, source_target_pairs={{0,2},{1,3},{2,4},{3,5},{4,6},{5,7},{6,8},{7,9},{8,10},{9,11},{10,... | collective-permute-start | bytes 3151880 | tf_op jit(solution)/shard_map/ppermute | solution.py:18
  535.3 78.4 %collective-permute-start.21 = (f32[114,2304]{1,0:T(8,128)}, f32[114,2304]{1,0:T(8,128)}, u32[]{:S(2)}, u32[]{:S(2)}) collective-permute-start(f32[114,2304]{1,0:T(8,128)} %get-tuple-element.47), channel_id=1, source_target_pairs={{0,1},{1,2},{2,3},{3,4},{4,5},{5,6},{6,7},{7,8},{8,9},{9,10},{10,1... | collective-permute-start | bytes 3151880 | tf_op jit(solution)/shard_map/ppermute | solution.py:18
  556.6 163.9 %all-gather.37.cloned.1.call-start = ((), (), s32[]{:S(2)}) async-start(), calls=%async_computation.15 | async-start | bytes 1382400 | tf_op jit(solution)/shard_map/all_gather | solution.py:52
  612.4 83.9 %collective-permute-start.17 = (f32[114,2304]{1,0:T(8,128)}, f32[114,2304]{1,0:T(8,128)}, u32[]{:S(2)}, u32[]{:S(2)}) collective-permute-start(f32[114,2304]{1,0:T(8,128)} %get-tuple-element.51), channel_id=1, source_target_pairs={{4,0},{5,1},{6,2},{7,3},{8,4},{9,5},{10,6},{11,7},{12,8},{13,9},{1... | collective-permute-start | bytes 3151880 | tf_op jit(solution)/shard_map/ppermute | solution.py:18
  613.7 83.9 %collective-permute-start.16 = (f32[114,2304]{1,0:T(8,128)}, f32[114,2304]{1,0:T(8,128)}, u32[]{:S(2)}, u32[]{:S(2)}) collective-permute-start(f32[114,2304]{1,0:T(8,128)} %get-tuple-element.52), channel_id=1, source_target_pairs={{5,0},{6,1},{7,2},{8,3},{9,4},{10,5},{11,6},{12,7},{13,8},{14,9},{... | collective-permute-start | bytes 3151880 | tf_op jit(solution)/shard_map/ppermute | solution.py:18
  615.0 82.6 %collective-permute-start.15 = (f32[114,2304]{1,0:T(8,128)}, f32[114,2304]{1,0:T(8,128)}, u32[]{:S(2)}, u32[]{:S(2)}) collective-permute-start(f32[114,2304]{1,0:T(8,128)} %get-tuple-element.53), channel_id=1, source_target_pairs={{6,0},{7,1},{8,2},{9,3},{10,4},{11,5},{12,6},{13,7},{14,8},{15,9},... | collective-permute-start | bytes 3151880 | tf_op jit(solution)/shard_map/ppermute | solution.py:18
  623.9 173.2 %all-gather.33.cloned.1.call-start = ((), (), s32[]{:S(2)}) async-start(), calls=%async_computation.13 | async-start | bytes 1382400 | tf_op jit(solution)/shard_map/all_gather | solution.py:50
  711.5 116.7 %all-gather.31.cloned.1.call-start = ((), (), s32[]{:S(2)}) async-start(), calls=%async_computation.12 | async-start | bytes 4147200 | tf_op jit(solution)/shard_map/all_gather | solution.py:49
  712.6 134.8 %all-gather.45.cloned.1.call-start = ((), (), s32[]{:S(2)}) async-start(), calls=%async_computation.19 | async-start | bytes 1382400 | tf_op jit(solution)/shard_map/all_gather | solution.py:52
  713.5 169.7 %all-gather.43.cloned.1.call-start = ((), (), s32[]{:S(2)}) async-start(), calls=%async_computation.18 | async-start | bytes 5222400 | tf_op jit(solution)/shard_map/all_gather | solution.py:51
  717.0 185.4 %all-gather.41.cloned.1.call-start = ((), (), s32[]{:S(2)}) async-start(), calls=%async_computation.17 | async-start | bytes 1382400 | tf_op jit(solution)/shard_map/all_gather | solution.py:50
  717.7 220.5 %all-gather.39.cloned.1.call-start = ((), (), s32[]{:S(2)}) async-start(), calls=%async_computation.16 | async-start | bytes 5222400 | tf_op jit(solution)/shard_map/all_gather | solution.py:49
  718.9 290.2 %reduce-scatter.7.cloned.1.call-start = ((), (), s32[]{:S(2)}) async-start(), calls=%async_computation.7 | async-start | bytes 1990656 | tf_op jit(solution)/shard_map/reduce_scatter | solution.py:68
  724.3 375.4 %reduce-scatter.5.cloned.1.call-start = ((), (), s32[]{:S(2)}) async-start(), calls=%async_computation.6 | async-start | bytes 4644864 | tf_op jit(solution)/shard_map/reduce_scatter | solution.py:67
  835.8 372.0 %reduce-scatter.11.cloned.1.call-start = ((), (), s32[]{:S(2)}) async-start(), calls=%async_computation.9 | async-start | bytes 5971968 | tf_op jit(solution)/shard_map/reduce_scatter | solution.py:68
  894.6 421.4 %reduce-scatter.9.cloned.1.call-start = ((), (), s32[]{:S(2)}) async-start(), calls=%async_computation.8 | async-start | bytes 5971968 | tf_op jit(solution)/shard_map/reduce_scatter | solution.py:67
  (77 other events, 2548.3 us)
Sparse Core Ops, SparseCore 0:
  9.5 58.5 all-gather.22
  69.7 59.2 all-gather.24
  130.6 116.8 all-gather.26
  248.8 68.5 all-gather.28
  556.7 44.4 all-gather.34
  623.9 48.2 all-gather.36
  711.6 85.4 all-gather.32
  798.7 29.4 all-gather.30
  830.3 17.0 all-gather.44
  848.8 34.3 all-gather.42
  885.3 17.0 all-gather.40
  903.8 34.3 all-gather.38
  942.2 66.7 reduce-scatter.6
  1013.0 86.6 reduce-scatter.4
  1103.7 104.0 reduce-scatter.10
  1211.8 104.1 reduce-scatter.8
where the time goes:
time: 1330 us; the launch traced here: 1320 us
  waiting for transfers between devices  806 us (61%)
  local copies, waits for them, and re-layouts  178 us (13%)
  starting transfers between devices  122 us (9%)
  matrix products  100 us (8%)
  other arithmetic  55.2 us (4%)
  blocking collectives  42.1 us (3%)
  between operations  18.6 us (1%)
    ppermute x28, waiting for transfers between devices, passed_along(): return lax.ppermute(block, axis, route)  245 us
    reduce_scatter x2, waiting for transfers between devices, replica_sums(): lax.psum_scatter(first_rows, 'rep', scatter_dimension=1, tiled=True)  199 us
    ppermute x28, starting transfers between devices, passed_along(): return lax.ppermute(block, axis, route)  122 us
    reduce_scatter x2, waiting for transfers between devices, replica_sums(): lax.psum_scatter(second_rows, 'rep', scatter_dimension=1, tiled=True)  117 us
    all_gather x2, waiting for transfers between devices, owned_grads(): lax.all_gather(right_one, 'grp', axis=0, tiled=True)  80.5 us
    all_gather x2, waiting for transfers between devices, owned_grads(): lax.all_gather(left_one, 'grp', axis=0, tiled=True)  62.8 us
    concatenate x1, local copies, waits for them, and re-layouts, per_device(): neighbours = jnp.concatenate(pieces, axis=0)  57.9 us
    unnamed x125, local copies, waits for them, and re-layouts  52.8 us
  transfers between devices with their start and end apart: 44, of which 26 were waited for; matrix products, arithmetic and copies ran while one was open for 16% of the time, Pallas kernels for 0%

commit v1 on v0

--- a/solution.py
+++ b/solution.py
@@ -47,7 +47,9 @@
 def owned_grads(left_one, right_one, left_two, right_two):
     all_left_one, all_right_one, all_left_two, all_right_two = (
         lax.all_gather(left_one, "grp", axis=0, tiled=True),
-        lax.all_gather(right_one, "grp", axis=0, tiled=True),
+        jnp.concatenate(
+            lax.all_to_all(jnp.stack([right_one] * lax.axis_size("grp")), "grp", 0, 0), axis=0
+        ),
         lax.all_gather(left_two, "grp", axis=0, tiled=True),
         lax.all_gather(right_two, "grp", axis=0, tiled=True),
     )

time: 1330 us -> 1310 us (0.985)
  waiting for transfers between devices: 806 us -> 688 us
  starting transfers between devices: 122 us -> 189 us
  blocking collectives: 42.1 us -> 71.8 us
    all_gather x2 -> x0, waiting for transfers between devices: 80.5 us -> none  [owned_grads(): lax.all_gather(right_one, 'grp', axis=0, tiled=True)]
    all_to_all x0 -> x1, starting transfers between devices: none -> 66.9 us  [owned_grads(): lax.all_to_all(jnp.stack([right_one] * lax.axis_size('grp')), 'grp', 0, 0)]
    all_gather x2, waiting for transfers between devices: 62.8 us -> 6.72 us  [owned_grads(): lax.all_gather(left_one, 'grp', axis=0, tiled=True)]
    all_to_all x0 -> x1, blocking collectives: none -> 30 us  [owned_grads(): lax.all_to_all(jnp.stack([right_one] * lax.axis_size('grp')), 'grp', 0, 0)]
    all_to_all x0 -> x1, waiting for transfers between devices: none -> 27.5 us  [owned_grads(): lax.all_to_all(jnp.stack([right_one] * lax.axis_size('grp')), 'grp', 0, 0)]
    unnamed x125 -> x133, local copies, waits for them, and re-layouts: 52.8 us -> 51.2 us
  transfers between devices with their start and end apart: 44 -> 43, of which waited for: 26 -> 25; matrix products, arithmetic and copies ran while one was open for 16% -> 17% of each run, Pallas kernels for 0% -> 0%
where the time goes in v1:
time: 1310 us; the launch traced here: 1300 us
  waiting for transfers between devices  688 us (53%)
  starting transfers between devices  189 us (14%)
  local copies, waits for them, and re-layouts  179 us (14%)
  matrix products  99.9 us (8%)
  blocking collectives  71.8 us (5%)
  other arithmetic  54.5 us (4%)
  between operations  18.8 us (1%)
    ppermute x28, waiting for transfers between devices, passed_along(): return lax.ppermute(block, axis, route)  245 us
    reduce_scatter x2, waiting for transfers between devices, replica_sums(): lax.psum_scatter(first_rows, 'rep', scatter_dimension=1, tiled=True)  199 us
    ppermute x28, starting transfers between devices, passed_along(): return lax.ppermute(block, axis, route)  121 us
    reduce_scatter x2, waiting for transfers between devices, replica_sums(): lax.psum_scatter(second_rows, 'rep', scatter_dimension=1, tiled=True)  111 us
    all_to_all x1, starting transfers between devices, owned_grads(): lax.all_to_all(jnp.stack([right_one] * lax.axis_size('grp')), 'grp', 0, 0)  66.9 us
    concatenate x1, local copies, waits for them, and re-layouts, per_device(): neighbours = jnp.concatenate(pieces, axis=0)  57.8 us
    all_gather x1, waiting for transfers between devices, per_device(): lax.all_gather(attn_in, 'grp', axis=0, tiled=True)  52.1 us
    unnamed x133, local copies, waits for them, and re-layouts  51.2 us
  transfers between devices with their start and end apart: 43, of which 25 were waited for; matrix products, arithmetic and copies ran while one was open for 17% of the time, Pallas kernels for 0%

profile of v1, /device:TPU:0, one launch (start us, length us, event | category | flops | bytes accessed | tf_op | source)
XLA Modules:
  0.0 1301.0 jit_solution(6315348791036982454)
XLA Ops:
  16.0 52.1 %all-gather.19.cloned.1.call-done = bf16[3456,1152]{1,0:T(8,128)(2,1)} async-done(((bf16[864,1152]{1,0:T(8,128)(2,1)}), bf16[3456,1152]{1,0:T(8,128)(2,1)}) %all-gather.19.cloned.1.call-update) | async-done | bytes 7962640 | tf_op jit(solution)/shard_map/all_gather | solution.py:117
  81.3 20.3 %collective-permute-done.13 = bf16[114,2304]{1,0:T(8,128)(2,1)S(1)} collective-permute-done((bf16[114,2304]{1,0:T(8,128)(2,1)S(1)}, bf16[114,2304]{1,0:T(8,128)(2,1)S(1)}, u32[]{:S(2)}, u32[]{:S(2)}) %collective-permute-start.13) | collective-permute-done | bytes 525344 | tf_op jit(solution)/shard_map/ppermute | solution.py:18
  106.9 13.9 %collective-permute-start.6 = (bf16[114,2304]{1,0:T(8,128)(2,1)S(1)}, bf16[114,2304]{1,0:T(8,128)(2,1)S(1)}, u32[]{:S(2)}, u32[]{:S(2)}) collective-permute-start(bf16[114,2304]{1,0:T(8,128)(2,1)S(1)} %slice.92), channel_id=1, source_target_pairs={{0,1},{1,2},{2,3},{3,4},{4,5},{5,6},{6,7},{7,8},{8,9},{9,10},{10,1... | collective-permute-start | bytes 1575944 | tf_op jit(solution)/shard_map/ppermute | solution.py:18
  134.1 17.1 %collective-permute-start.3 = (bf16[114,2304]{1,0:T(8,128)(2,1)S(1)}, bf16[114,2304]{1,0:T(8,128)(2,1)}, u32[]{:S(2)}, u32[]{:S(2)}) collective-permute-start(bf16[114,2304]{1,0:T(8,128)(2,1)S(1)} %slice.92), channel_id=1, source_target_pairs={{0,4},{1,5},{2,6},{3,7},{4,8},{5,9},{6,10},{7,11},{8,12},{9,13},{1... | collective-permute-start | bytes 1575944 | tf_op jit(solution)/shard_map/ppermute | solution.py:18
  155.1 28.4 %collective-permute-start.1 = (bf16[114,2304]{1,0:T(8,128)(2,1)S(1)}, bf16[114,2304]{1,0:T(8,128)(2,1)}, u32[]{:S(2)}, u32[]{:S(2)}) collective-permute-start(bf16[114,2304]{1,0:T(8,128)(2,1)S(1)} %slice.92), channel_id=1, source_target_pairs={{0,6},{1,7},{2,8},{3,9},{4,10},{5,11},{6,12},{7,13},{8,14},{9,15},... | collective-permute-start | bytes 1575944 | tf_op jit(solution)/shard_map/ppermute | solution.py:18
  194.2 19.4 %collective-permute-done.1 = bf16[114,2304]{1,0:T(8,128)(2,1)} collective-permute-done((bf16[114,2304]{1,0:T(8,128)(2,1)S(1)}, bf16[114,2304]{1,0:T(8,128)(2,1)}, u32[]{:S(2)}, u32[]{:S(2)}) %collective-permute-start.1) | collective-permute-done | bytes 525344 | tf_op jit(solution)/shard_map/ppermute | solution.py:18
  213.6 21.3 %collective-permute-done = bf16[114,2304]{1,0:T(8,128)(2,1)} collective-permute-done((bf16[114,2304]{1,0:T(8,128)(2,1)S(1)}, bf16[114,2304]{1,0:T(8,128)(2,1)}, u32[]{:S(2)}, u32[]{:S(2)}) %collective-permute-start) | collective-permute-done | bytes 525344 | tf_op jit(solution)/shard_map/ppermute | solution.py:18
  234.9 57.8 %concatenate.14 = bf16[1710,2304]{1,0:T(8,128)(2,1)} concatenate(bf16[114,2304]{1,0:T(8,128)(2,1)} %collective-permute-done, bf16[114,2304]{1,0:T(8,128)(2,1)} %collective-permute-done.1, bf16[114,2304]{1,0:T(8,128)(2,1)} %collective-permute-done.2, bf16[114,2304]{1,0:T(8,128)(2,1)} %collective-permute-done.3, bf16[114,2304]{1,0:T(8,128)(2,1)} %collective-permute-done.4, ...), dimensions={0} | concatenate | bytes 15759360 | tf_op jit(solution)/shard_map/concatenate | solution.py:135
  292.7 18.3 %gather_fusion = bf16[1458,2304]{1,0:T(8,128)(2,1)} fusion(bf16[1710,2304]{1,0:T(8,128)(2,1)} %concatenate.14, s32[2048]{0:T(1024)S(1)} %pad_clamp_fusion), kind=kCustom, calls=%fused_computation | custom fusion | bytes 13442760 | tf_op jit(solution)/shard_map/gather | solution.py:136
  436.6 30.0 %scatter_custom_fusion = f32[1710,2304]{1,0:T(8,128)} fusion(s32[1458]{0:T(1024)} %copy-done.43, f32[1458,1152]{1,0:T(8,128)} %copy.60, f32[]{:T(128)} %constant.83.clone.1, f32[1458,1152]{1,0:T(8,128)} %copy.59, f32[]{:T(128)} %constant.37.clone.1), kind=kCustom, calls=%fused_computation.2 | custom fusion | flops 6718464 | bytes 29252608 | tf_op jit(solution)/shard_map/scatter-add | solution.py:194
  497.1 13.1 %collective-permute-done.27 = f32[114,2304]{1,0:T(8,128)S(1)} collective-permute-done((f32[114,2304]{1,0:T(8,128)S(1)}, f32[114,2304]{1,0:T(8,128)S(1)}, u32[]{:S(2)}, u32[]{:S(2)}) %collective-permute-start.27) | collective-permute-done | bytes 1050656 | tf_op jit(solution)/shard_map/ppermute | solution.py:18
  512.5 21.4 %collective-permute-done.26 = f32[114,2304]{1,0:T(8,128)S(1)} collective-permute-done((f32[114,2304]{1,0:T(8,128)S(1)}, f32[114,2304]{1,0:T(8,128)S(1)}, u32[]{:S(2)}, u32[]{:S(2)}) %collective-permute-start.26) | collective-permute-done | bytes 1050656 | tf_op jit(solution)/shard_map/ppermute | solution.py:18
  536.2 16.0 %collective-permute-done.25 = f32[114,2304]{1,0:T(8,128)S(1)} collective-permute-done((f32[114,2304]{1,0:T(8,128)S(1)}, f32[114,2304]{1,0:T(8,128)S(1)}, u32[]{:S(2)}, u32[]{:S(2)}) %collective-permute-start.25) | collective-permute-done | bytes 1050656 | tf_op jit(solution)/shard_map/ppermute | solution.py:18
  555.4 20.5 %collective-permute-done.24 = f32[114,2304]{1,0:T(8,128)} collective-permute-done((f32[114,2304]{1,0:T(8,128)}, f32[114,2304]{1,0:T(8,128)}, u32[]{:S(2)}, u32[]{:S(2)}) %collective-permute-start.24) | collective-permute-done | bytes 1050656 | tf_op jit(solution)/shard_map/ppermute | solution.py:18
  578.6 32.5 %collective-permute-done.22 = f32[114,2304]{1,0:T(8,128)} collective-permute-done((f32[114,2304]{1,0:T(8,128)}, f32[114,2304]{1,0:T(8,128)}, u32[]{:S(2)}, u32[]{:S(2)}) %collective-permute-start.22) | collective-permute-done | bytes 1050656 | tf_op jit(solution)/shard_map/ppermute | solution.py:18
  633.5 61.3 %collective-permute-done.17 = f32[114,2304]{1,0:T(8,128)} collective-permute-done((f32[114,2304]{1,0:T(8,128)}, f32[114,2304]{1,0:T(8,128)}, u32[]{:S(2)}, u32[]{:S(2)}) %collective-permute-start.17) | collective-permute-done | bytes 1050656 | tf_op jit(solution)/shard_map/ppermute | solution.py:18
  717.9 66.9 %all-to-all-start = ((bf16[4,114,1152]{2,1,0:T(8,128)(2,1)}), bf16[4,114,1152]{2,1,0:T(8,128)(2,1)S(1)}, u32[]{:S(2)}, u32[]{:S(2)}) async-start(bf16[4,114,1152]{2,1,0:T(8,128)(2,1)} %stack.10), calls=%async_computation | async-start | bytes 2211840 | tf_op jit(solution)/shard_map/all_to_all | solution.py:51
  784.8 27.5 %all-to-all-done = bf16[4,114,1152]{2,1,0:T(8,128)(2,1)S(1)} async-done(((bf16[4,114,1152]{2,1,0:T(8,128)(2,1)}), bf16[4,114,1152]{2,1,0:T(8,128)(2,1)S(1)}, u32[]{:S(2)}, u32[]{:S(2)}) %all-to-all-start) | async-done | bytes 1050656 | tf_op jit(solution)/shard_map/all_to_all | solution.py:51
  834.0 34.4 %all-gather.35.cloned.1.call-done = bf16[4,114,4304]{2,1,0:T(8,128)(2,1)} async-done(((bf16[1,114,4304]{2,1,0:T(8,128)(2,1)}), bf16[4,114,4304]{2,1,0:T(8,128)(2,1)}) %all-gather.35.cloned.1.call-update) | async-done | bytes 3925264 | tf_op jit(solution)/shard_map/all_gather | solution.py:53
  881.1 30.0 %all_to_all.10 = bf16[4,114,1152]{2,1,0:T(8,128)(2,1)S(1)} all-to-all(bf16[4,114,1152]{2,1,0:T(8,128)(2,1)S(1)} %stack.27), channel_id=1, replica_groups=mesh['rep'=8,'grp'=4] {'grp'}, dimensions={0} | all-to-all | bytes 2101248 | tf_op jit(solution)/shard_map/all_to_all | solution.py:51
  942.2 41.9 %all-reduce = (f32[1152]{0:T(1024)}, f32[1152]{0:T(1024)}, f32[2,1152]{1,0:T(2,128)}, f32[1152]{0:T(1024)}, f32[1152]{0:T(1024)}, /*index=5*/f32[1152]{0:T(1024)}, f32[4304]{0:T(1024)}, f32[1152]{0:T(1024)}) all-reduce(f32[1152]{0:T(1024)S(1)} %get-tuple-element.16, ...), channel_id=1, replica_groups=mesh['rep'=8,'grp'=4] {'rep','grp'}, use_global_device_ids=true, to_apply=%region_16.17 | all-reduce | flops 13520 | bytes 108160 | tf_op jit(solution)/shard_map/psum | solution.py:209
  986.6 90.9 %reduce-scatter.5.cloned.1.call-done = f32[864,144]{0,1:T(8,128)} async-done(((f32[864,1152]{0,1:T(8,128)}), f32[864,144]{0,1:T(8,128)}) %reduce-scatter.5.cloned.1.call-update) | async-done | bytes 497680 | tf_op jit(solution)/shard_map/reduce_scatter | solution.py:69
  1077.5 108.3 %reduce-scatter.11.cloned.1.call-done = f32[1076,144]{0,1:T(8,128)} async-done(((f32[1076,1152]{0,1:T(8,128)}), f32[1076,144]{0,1:T(8,128)}) %reduce-scatter.11.cloned.1.call-update) | async-done | bytes 619792 | tf_op jit(solution)/shard_map/reduce_scatter | solution.py:70
  1185.8 108.2 %reduce-scatter.9.cloned.1.call-done = f32[1076,144]{0,1:T(8,128)} async-done(((f32[1076,1152]{0,1:T(8,128)}), f32[1076,144]{0,1:T(8,128)}) %reduce-scatter.9.cloned.1.call-update) | async-done | bytes 619792 | tf_op jit(solution)/shard_map/reduce_scatter | solution.py:69
  (301 shorter events, 330.7 us)
Async XLA Ops:
  7.9 333.5 %all-gather.21.cloned.1.call-start = ((), (), s32[]{:S(2)}) async-start(), calls=%async_computation.7 | async-start | bytes 3317760 | tf_op jit(solution)/shard_map/all_gather | solution.py:118
  8.7 335.8 %all-gather.23.cloned.1.call-start = ((), (), s32[]{:S(2)}) async-start(), calls=%async_computation.12 | async-start | bytes 12441600 | tf_op jit(solution)/shard_map/all_gather | solution.py:119
  9.4 354.1 %all-gather.25.cloned.1.call-start = ((), (), s32[]{:S(2)}) async-start(), calls=%async_computation.13 | async-start | bytes 12441600 | tf_op jit(solution)/shard_map/all_gather | solution.py:120
  10.0 701.4 %all-gather.29.cloned.1.call-start = ((), (), s32[]{:S(2)}) async-start(), calls=%async_computation.15 | async-start | bytes 1382400 | tf_op jit(solution)/shard_map/all_gather | solution.py:53
  120.8 62.7 %collective-permute-start.5 = (bf16[114,2304]{1,0:T(8,128)(2,1)S(1)}, bf16[114,2304]{1,0:T(8,128)(2,1)S(1)}, u32[]{:S(2)}, u32[]{:S(2)}) collective-permute-start(bf16[114,2304]{1,0:T(8,128)(2,1)S(1)} %slice.92), channel_id=1, source_target_pairs={{0,2},{1,3},{2,4},{3,5},{4,6},{5,7},{6,8},{7,9},{8,10},{9,11},{10,... | collective-permute-start | bytes 1575944 | tf_op jit(solution)/shard_map/ppermute | solution.py:18
  128.2 66.0 %collective-permute-start.4 = (bf16[114,2304]{1,0:T(8,128)(2,1)S(1)}, bf16[114,2304]{1,0:T(8,128)(2,1)}, u32[]{:S(2)}, u32[]{:S(2)}) collective-permute-start(bf16[114,2304]{1,0:T(8,128)(2,1)S(1)} %slice.92), channel_id=1, source_target_pairs={{0,3},{1,4},{2,5},{3,6},{4,7},{5,8},{6,9},{7,10},{8,11},{9,12},{10... | collective-permute-start | bytes 1575944 | tf_op jit(solution)/shard_map/ppermute | solution.py:18
  485.1 67.1 %collective-permute-start.25 = (f32[114,2304]{1,0:T(8,128)S(1)}, f32[114,2304]{1,0:T(8,128)S(1)}, u32[]{:S(2)}, u32[]{:S(2)}) collective-permute-start(f32[114,2304]{1,0:T(8,128)S(1)} %get-tuple-element.43), channel_id=1, source_target_pairs={{0,5},{1,6},{2,7},{3,8},{4,9},{5,10},{6,11},{7,12},{8,13},{9,14},{... | collective-permute-start | bytes 3151880 | tf_op jit(solution)/shard_map/ppermute | solution.py:18
  486.5 89.5 %collective-permute-start.24 = (f32[114,2304]{1,0:T(8,128)}, f32[114,2304]{1,0:T(8,128)}, u32[]{:S(2)}, u32[]{:S(2)}) collective-permute-start(f32[114,2304]{1,0:T(8,128)} %get-tuple-element.44), channel_id=1, source_target_pairs={{0,4},{1,5},{2,6},{3,7},{4,8},{5,9},{6,10},{7,11},{8,12},{9,13},{1... | collective-permute-start | bytes 3151880 | tf_op jit(solution)/shard_map/ppermute | solution.py:18
  494.8 82.5 %collective-permute-start.23 = (f32[114,2304]{1,0:T(8,128)}, f32[114,2304]{1,0:T(8,128)}, u32[]{:S(2)}, u32[]{:S(2)}) collective-permute-start(f32[114,2304]{1,0:T(8,128)} %get-tuple-element.45), channel_id=1, source_target_pairs={{0,3},{1,4},{2,5},{3,6},{4,7},{5,8},{6,9},{7,10},{8,11},{9,12},{10... | collective-permute-start | bytes 3151880 | tf_op jit(solution)/shard_map/ppermute | solution.py:18
  510.2 100.8 %collective-permute-start.22 = (f32[114,2304]{1,0:T(8,128)}, f32[114,2304]{1,0:T(8,128)}, u32[]{:S(2)}, u32[]{:S(2)}) collective-permute-start(f32[114,2304]{1,0:T(8,128)} %get-tuple-element.46), channel_id=1, source_target_pairs={{0,2},{1,3},{2,4},{3,5},{4,6},{5,7},{6,8},{7,9},{8,10},{9,11},{10,... | collective-permute-start | bytes 3151880 | tf_op jit(solution)/shard_map/ppermute | solution.py:18
  533.9 78.4 %collective-permute-start.21 = (f32[114,2304]{1,0:T(8,128)}, f32[114,2304]{1,0:T(8,128)}, u32[]{:S(2)}, u32[]{:S(2)}) collective-permute-start(f32[114,2304]{1,0:T(8,128)} %get-tuple-element.47), channel_id=1, source_target_pairs={{0,1},{1,2},{2,3},{3,4},{4,5},{5,6},{6,7},{7,8},{8,9},{9,10},{10,1... | collective-permute-start | bytes 3151880 | tf_op jit(solution)/shard_map/ppermute | solution.py:18
  555.4 157.5 %all-gather.31.cloned.1.call-start = ((), (), s32[]{:S(2)}) async-start(), calls=%async_computation.16 | async-start | bytes 1382400 | tf_op jit(solution)/shard_map/all_gather | solution.py:54
  611.1 83.7 %collective-permute-start.17 = (f32[114,2304]{1,0:T(8,128)}, f32[114,2304]{1,0:T(8,128)}, u32[]{:S(2)}, u32[]{:S(2)}) collective-permute-start(f32[114,2304]{1,0:T(8,128)} %get-tuple-element.51), channel_id=1, source_target_pairs={{4,0},{5,1},{6,2},{7,3},{8,4},{9,5},{10,6},{11,7},{12,8},{13,9},{1... | collective-permute-start | bytes 3151880 | tf_op jit(solution)/shard_map/ppermute | solution.py:18
  612.4 83.8 %collective-permute-start.16 = (f32[114,2304]{1,0:T(8,128)}, f32[114,2304]{1,0:T(8,128)}, u32[]{:S(2)}, u32[]{:S(2)}) collective-permute-start(f32[114,2304]{1,0:T(8,128)} %get-tuple-element.52), channel_id=1, source_target_pairs={{5,0},{6,1},{7,2},{8,3},{9,4},{10,5},{11,6},{12,7},{13,8},{14,9},{... | collective-permute-start | bytes 3151880 | tf_op jit(solution)/shard_map/ppermute | solution.py:18
  613.7 82.5 %collective-permute-start.15 = (f32[114,2304]{1,0:T(8,128)}, f32[114,2304]{1,0:T(8,128)}, u32[]{:S(2)}, u32[]{:S(2)}) collective-permute-start(f32[114,2304]{1,0:T(8,128)} %get-tuple-element.53), channel_id=1, source_target_pairs={{6,0},{7,1},{8,2},{9,3},{10,4},{11,5},{12,6},{13,7},{14,8},{15,9},... | collective-permute-start | bytes 3151880 | tf_op jit(solution)/shard_map/ppermute | solution.py:18
  622.5 193.0 %all-gather.27.cloned.1.call-start = ((), (), s32[]{:S(2)}) async-start(), calls=%async_computation.14 | async-start | bytes 4147200 | tf_op jit(solution)/shard_map/all_gather | solution.py:49
  705.7 126.7 %all-gather.37.cloned.1.call-start = ((), (), s32[]{:S(2)}) async-start(), calls=%async_computation.19 | async-start | bytes 1382400 | tf_op jit(solution)/shard_map/all_gather | solution.py:54
  706.6 161.8 %all-gather.35.cloned.1.call-start = ((), (), s32[]{:S(2)}) async-start(), calls=%async_computation.18 | async-start | bytes 5222400 | tf_op jit(solution)/shard_map/all_gather | solution.py:53
  710.1 206.0 %all-gather.33.cloned.1.call-start = ((), (), s32[]{:S(2)}) async-start(), calls=%async_computation.17 | async-start | bytes 5222400 | tf_op jit(solution)/shard_map/all_gather | solution.py:49
  711.3 275.3 %reduce-scatter.7.cloned.1.call-start = ((), (), s32[]{:S(2)}) async-start(), calls=%async_computation.9 | async-start | bytes 1990656 | tf_op jit(solution)/shard_map/reduce_scatter | solution.py:70
  717.9 94.4 %all-to-all-start = ((bf16[4,114,1152]{2,1,0:T(8,128)(2,1)}), bf16[4,114,1152]{2,1,0:T(8,128)(2,1)S(1)}, u32[]{:S(2)}, u32[]{:S(2)}) async-start(bf16[4,114,1152]{2,1,0:T(8,128)(2,1)} %stack.10), calls=%async_computation | async-start | bytes 2211840 | tf_op jit(solution)/shard_map/all_to_all | solution.py:51
  784.8 292.7 %reduce-scatter.5.cloned.1.call-start = ((), (), s32[]{:S(2)}) async-start(), calls=%async_computation.8 | async-start | bytes 4644864 | tf_op jit(solution)/shard_map/reduce_scatter | solution.py:69
  823.0 362.8 %reduce-scatter.11.cloned.1.call-start = ((), (), s32[]{:S(2)}) async-start(), calls=%async_computation.11 | async-start | bytes 5971968 | tf_op jit(solution)/shard_map/reduce_scatter | solution.py:70
  880.1 413.9 %reduce-scatter.9.cloned.1.call-start = ((), (), s32[]{:S(2)}) async-start(), calls=%async_computation.10 | async-start | bytes 5971968 | tf_op jit(solution)/shard_map/reduce_scatter | solution.py:69
  (81 other events, 2034.6 us)
Sparse Core Ops, SparseCore 0:
  9.5 58.5 all-gather.18
  69.7 59.2 all-gather.20
  130.6 116.7 all-gather.22
  248.8 68.6 all-gather.24
  555.5 44.1 all-gather.28
  622.6 47.9 all-gather.30
  705.8 109.6 all-gather.26
  817.7 14.7 all-gather.36
  834.0 34.3 all-gather.34
  869.8 46.2 all-gather.32
  920.1 66.4 reduce-scatter.6
  990.6 86.8 reduce-scatter.4
  1081.7 104.1 reduce-scatter.10
  1189.8 104.1 reduce-scatter.8
